TPU v7x, 256 devices: a whole 4x4x8 slice. The times are simulated.
256 devices in a mesh: seq: 64 (over y, z, core), tp: 4 (over x).
Axes of the slice: x: 4, y: 4, z: 8, core: 2. Of those that a mesh axis runs over, the one named last changes fastest.
Arguments:
- normed_input: bfloat16 [32768, 5376], P('seq', 'tp'), may hold values from -6 to 6
- query: bfloat16 [32768, 4096], P('seq', 'tp'), may hold values from -220 to 220, as said below
- key: bfloat16 [32768, 2048], P('seq', 'tp'), may hold values from -7 to 7
- value: bfloat16 [32768, 2048], P('seq', 'tp'), may hold values from -6 to 6
- adapter_down_maps: bfloat16 [64, 16, 5376], P(None, None, 'tp'), may hold values from -0.078125 to 0.078125
- adapter_up_maps: bfloat16 [64, 16, 2048], P(None, None, 'tp'), may hold values from -1.5 to 1.5
- block_adapter_choice: int32 [16], replicated, may hold values from 0 to 63
Outputs:
- attended: bfloat16 [32768, 4096], P('seq', 'tp')
Inputs may be any that keep to these rules, and one draw needn't show every extreme that they name: `query`: queries; some may be aligned with nearby keys.
All inputs are finite; a program needn't handle non-finite values.
Results may differ from a plain program's by a relative error of at most 0.014.
Values may be sent and summed in bfloat16 or wider, within the bound.
A program may use at most 128 MiB of HBM per device.

v0:
```python
import jax
import jax.numpy as jnp
from jax import lax
from jax.sharding import PartitionSpec as P

HEAD_WIDTH = 128
WINDOW = 1024
ADAPTER_RANK = 16
SEG_LEN = 2048
query_scale = 168.0 ** (-0.5)


def shifted(value, axis, steps):
    count = lax.axis_size(axis)
    leading, last = (max(0, -steps), min(count, count - steps))
    return lax.ppermute(value, axis, [(source, source + steps) for source in range(leading, last)])


def on_device(
    normed_input, query, key, value, adapter_down_maps, adapter_up_maps, block_adapter_choice
):
    tok = query.shape[0]
    columns = key.shape[1]
    kv_local = columns // HEAD_WIDTH
    q_local = query.shape[1] // HEAD_WIDTH
    group = q_local // kv_local
    where_seq = lax.axis_index("seq")
    blk = min(tok, SEG_LEN)
    nblk = tok // blk
    last_seg = block_adapter_choice.shape[0] - 1
    token_rows = where_seq * tok + jnp.arange(nblk, dtype=jnp.int32) * blk
    segment_adapter_ids = block_adapter_choice[jnp.clip(token_rows // SEG_LEN, 0, last_seg)]
    selected_down = adapter_down_maps[segment_adapter_ids]
    partial_value = jnp.einsum(
        "bsd,brd->bsr",
        normed_input.reshape(nblk, blk, -1),
        selected_down,
        preferred_element_type=jnp.float32,
    )
    rank_activation = lax.psum(partial_value.reshape(tok, ADAPTER_RANK).astype(jnp.bfloat16), "tp")
    hops = WINDOW // tok
    selected_up = adapter_up_maps[segment_adapter_ids]
    value_update = jnp.einsum(
        "bsr,brc->bsc",
        rank_activation.reshape(nblk, blk, ADAPTER_RANK),
        selected_up,
        preferred_element_type=jnp.float32,
    )
    value_full = (value + value_update.reshape(tok, columns)).astype(jnp.bfloat16)
    pieces = []
    current = (key, value_full)
    for step in range(hops):
        current = shifted((current[0], current[1]), "seq", 1)
        pieces.append((step + 1, current))
    received = pieces[::-1]
    rim_keys = [piece[1][0] for piece in received]
    rim_vals = [piece[1][1] for piece in received]
    keys_all = jnp.concatenate(rim_keys + [key], axis=0)
    vals_all = jnp.concatenate(rim_vals + [value_full], axis=0)
    qblock = min(512, tok)
    span = qblock + WINDOW
    start_global = where_seq * tok

    def one_block(index):
        first = index * qblock
        qrows = query.reshape(qblock, kv_local, group, HEAD_WIDTH)
        krows = keys_all.reshape(span, kv_local, HEAD_WIDTH)
        vrows = vals_all.reshape(span, kv_local, HEAD_WIDTH)
        scores = (
            jnp.einsum("qkgd,lkd->kgql", qrows, krows, preferred_element_type=jnp.float32)
            * query_scale
        )
        qpos = start_global + first + jnp.arange(qblock, dtype=jnp.int32)[:, None]
        kpos = start_global + first - WINDOW + jnp.arange(span, dtype=jnp.int32)[None, :]
        usable = (kpos <= qpos) & (qpos - kpos < WINDOW) & (kpos >= 0)
        scores = jnp.where(usable, scores, -1e30)
        top = jnp.max(scores, axis=-1, keepdims=True)
        expo = jnp.exp(scores - top)
        weights = (expo / jnp.sum(expo, axis=-1, keepdims=True)).astype(jnp.bfloat16)
        out = jnp.einsum("kgql,lkd->qkgd", weights, vrows, preferred_element_type=jnp.float32)
        return out.astype(jnp.bfloat16).reshape(qblock, q_local * HEAD_WIDTH)

    blocks = lax.map(one_block, jnp.arange(tok // qblock, dtype=jnp.int32))
    return blocks.reshape(tok, q_local * HEAD_WIDTH)


def solution(mesh):
    placed = (
        P("seq", "tp"),
        P("seq", "tp"),
        P("seq", "tp"),
        P("seq", "tp"),
        P(None, None, "tp"),
        P(None, None, "tp"),
        P(),
    )
    return jax.shard_map(
        on_device, mesh=mesh, in_specs=placed, out_specs=P("seq", "tp"), check_vma=False
    )
```

profile of v0, /device:TPU:16, one launch (start us, length us, event | category | flops | bytes accessed | tf_op | source)
XLA Modules:
  0.0 97.9 jit_solution(14657647938584223890)
XLA Ops:
  0.0 0.0 copy-start
  0.0 1.4 %dynamic-slice.8 = s32[1]{0:T(128)} dynamic-slice(s32[16]{0:T(128)} %param.13, s32[]{:T(128)} %bitcast.1), dynamic_slice_sizes={1} | dynamic-slice | bytes 12 | tf_op jit(solution)/shard_map/gather | solution.py:32
  3.1 0.0 copy-done
  3.1 1.6 %fusion.12 = bf16[512,16]{0,1:T(8,128)(2,1)S(1)} fusion(bf16[512,1344]{0,1:T(8,128)(2,1)} %param.7, bf16[64,16,1344]{2,1,0:T(8,128)(2,1)S(1)} %copy-done, s32[]{:T(128)} %bitcast.2), kind=kOutput, calls=%fused_computation.19 | convolution fusion | flops 22028288 | bytes 1437700 | tf_op jit(solution)/shard_map/bsd,brd->bsr/dot_general | solution.py:34
  4.7 16.9 %psum.7 = bf16[512,16]{0,1:T(8,128)(2,1)S(1)} all-reduce(bf16[512,16]{0,1:T(8,128)(2,1)S(1)} %fusion.12), channel_id=1, replica_groups=mesh['seq'=64,'tp'=4] {'tp'}, use_global_device_ids=true, to_apply=%region_0.1 | all-reduce | flops 8192 | bytes 32768 | tf_op jit(solution)/shard_map/psum | solution.py:40
  21.6 2.2 %fusion.11 = bf16[512,512]{1,0:T(8,128)(2,1)} fusion(bf16[512,16]{0,1:T(8,128)(2,1)S(1)} %psum.7, bf16[512,512]{1,0:T(8,128)(2,1)} %param.10, bf16[64,16,512]{2,1,0:T(8,128)(2,1)} %param.12, s32[]{:T(128)} %bitcast.2), kind=kOutput, calls=%fused_computation.17 | convolution fusion | flops 9175040 | bytes 1081856 | tf_op jit(solution)/shard_map/bsr,brc->bsc/dot_general | solution.py:43
  23.8 1.9 %collective-permute-start = (bf16[512,512]{1,0:T(8,128)(2,1)}, bf16[512,512]{1,0:T(8,128)(2,1)}, u32[]{:S(2)}, u32[]{:S(2)}) collective-permute-start(bf16[512,512]{1,0:T(8,128)(2,1)} %fusion.11), channel_id=1, source_target_pairs={{0,4},{4,8},{8,12},{12,16},{16,20},{20,24},{24,28},{28,32},{32,36}... | collective-permute-start | bytes 1572872 | tf_op jit(solution)/shard_map/ppermute | solution.py:16
  25.7 1.3 %copy.12 = bf16[512,512]{0,1:T(8,128)(2,1)S(1)} copy(bf16[512,512]{1,0:T(8,128)(2,1)} %param.9) | data formatting | bytes 1048576 | tf_op args[2]
  27.0 3.9 %collective-permute-start.2 = (bf16[512,512]{0,1:T(8,128)(2,1)S(1)}, bf16[512,512]{0,1:T(8,128)(2,1)}, u32[]{:S(2)}, u32[]{:S(2)}) collective-permute-start(bf16[512,512]{0,1:T(8,128)(2,1)S(1)} %copy.12), channel_id=1, source_target_pairs={{0,4},{4,8},{8,12},{12,16},{16,20},{20,24},{24,28},{28,32},{32,36}... | collective-permute-start | bytes 1572872 | tf_op jit(solution)/shard_map/ppermute | solution.py:16
  30.9 5.8 %collective-permute-done = bf16[512,512]{1,0:T(8,128)(2,1)} collective-permute-done((bf16[512,512]{1,0:T(8,128)(2,1)}, bf16[512,512]{1,0:T(8,128)(2,1)}, u32[]{:S(2)}, u32[]{:S(2)}) %collective-permute-start) | collective-permute-done | bytes 524320 | tf_op jit(solution)/shard_map/ppermute | solution.py:16
  36.7 1.9 %collective-permute-start.1 = (bf16[512,512]{1,0:T(8,128)(2,1)}, bf16[512,512]{1,0:T(8,128)(2,1)}, u32[]{:S(2)}, u32[]{:S(2)}) collective-permute-start(bf16[512,512]{1,0:T(8,128)(2,1)} %collective-permute-done), channel_id=1, source_target_pairs={{0,4},{4,8},{8,12},{12,16},{16,20},{20,24},{24,28},{28,32},{32,36}... | collective-permute-start | bytes 1572872 | tf_op jit(solution)/shard_map/ppermute | solution.py:16
  38.6 2.6 %reshape.60 = bf16[512,4,2,128]{3,2,1,0:T(2,128)(2,1)} reshape(bf16[512,1024]{1,0:T(8,128)(2,1)} %param.8) | data formatting | bytes 2097152 | tf_op jit(solution)/shard_map/while/body/eval_jaxpr/reshape | solution.py:66
  41.2 1.1 %collective-permute-done.2 = bf16[512,512]{0,1:T(8,128)(2,1)} collective-permute-done((bf16[512,512]{0,1:T(8,128)(2,1)S(1)}, bf16[512,512]{0,1:T(8,128)(2,1)}, u32[]{:S(2)}, u32[]{:S(2)}) %collective-permute-start.2) | collective-permute-done | bytes 524320 | tf_op jit(solution)/shard_map/ppermute | solution.py:16
  42.3 1.9 %collective-permute-start.3 = (bf16[512,512]{0,1:T(8,128)(2,1)}, bf16[512,512]{0,1:T(8,128)(2,1)}, u32[]{:S(2)}, u32[]{:S(2)}) collective-permute-start(bf16[512,512]{0,1:T(8,128)(2,1)} %collective-permute-done.2), channel_id=1, source_target_pairs={{0,4},{4,8},{8,12},{12,16},{16,20},{20,24},{24,28},{28,32},{32,36}... | collective-permute-start | bytes 1572872 | tf_op jit(solution)/shard_map/ppermute | solution.py:16
  44.3 1.9 %fusion.9 = pred[512,1536]{0,1:T(8,128)(4,1)} fusion(s32[512]{0:T(512)S(1)} %iota_add_fusion.1, s32[1536]{0:T(1024)S(1)} %iota_add_fusion, pred[1536]{0:T(1024)(128)(4,1)S(1)} %broadcast_compare_fusion), kind=kLoop, calls=%fused_computation.12 | loop fusion | flops 3932160 | bytes 796160 | tf_op jit(solution)/shard_map/while/body/eval_jaxpr/and | solution.py:75
  46.2 3.5 %collective-permute-done.1 = bf16[512,512]{1,0:T(8,128)(2,1)} collective-permute-done((bf16[512,512]{1,0:T(8,128)(2,1)}, bf16[512,512]{1,0:T(8,128)(2,1)}, u32[]{:S(2)}, u32[]{:S(2)}) %collective-permute-start.1) | collective-permute-done | bytes 524320 | tf_op jit(solution)/shard_map/ppermute | solution.py:16
  49.6 2.6 %pad_maximum_fusion = bf16[1536,512]{1,0:T(8,128)(2,1)} fusion(bf16[512,512]{1,0:T(8,128)(2,1)} %fusion.11, bf16[512,512]{1,0:T(8,128)(2,1)} %collective-permute-done, bf16[512,512]{1,0:T(8,128)(2,1)} %collective-permute-done.1), kind=kLoop, calls=%fused_computation.13 | loop fusion | flops 4718592 | bytes 3145728 | tf_op jit(solution)/shard_map/concatenate | solution.py:59
  52.2 2.6 %copy.22 = bf16[1536,512]{0,1:T(8,128)(2,1)} copy(bf16[1536,512]{1,0:T(8,128)(2,1)} %pad_maximum_fusion) | data formatting | bytes 3145728 | tf_op jit(solution)/shard_map/while/body/eval_jaxpr/reshape | solution.py:68
  54.9 0.0 copy-start.2
  54.9 0.4 collective-permute-done.3
  55.3 1.3 %pad_maximum_fusion.1 = bf16[1536,512]{0,1:T(8,128)(2,1)S(1)} fusion(bf16[512,512]{0,1:T(8,128)(2,1)S(1)} %copy.12, bf16[512,512]{0,1:T(8,128)(2,1)} %collective-permute-done.2, bf16[512,512]{0,1:T(8,128)(2,1)} %collective-permute-done.3), kind=kLoop, calls=%fused_computation.14 | loop fusion | flops 4718592 | bytes 3145728 | tf_op jit(solution)/shard_map/concatenate | solution.py:58
  56.6 0.0 copy-start.1
  56.6 1.1 %copy-done.1 = bf16[1536,512]{0,1:T(8,128)(2,1)} copy-done((bf16[1536,512]{0,1:T(8,128)(2,1)}, bf16[1536,512]{0,1:T(8,128)(2,1)S(1)}, u32[]{:S(2)}) %copy-start.1) | copy-done | bytes 1572888
  57.7 0.0 copy-done.2
  57.7 11.8 %fusion.15 = f32[4,1536,512,2]{2,1,3,0:T(8,128)} fusion(bf16[1536,4,128,1]{0,2,3,1:T(8,128)(2,1)S(1)} %bitcast.42, bf16[512,4,2,128]{3,2,1,0:T(2,128)(2,1)S(1)} %copy-done.2), kind=kOutput, calls=%fused_computation.21 | convolution fusion | flops 1610612736 | bytes 27787264 | tf_op jit(solution)/shard_map/while/body/eval_jaxpr/qkgd,lkd->kgql/dot_general | solution.py:70
  69.5 10.9 %fusion.30 = f32[4,2,512]{2,1,0:T(2,128)S(1)} fusion(pred[512,1536]{0,1:T(8,128)(4,1)} %fusion.9, bf16[1536,4,128,1]{0,2,3,1:T(8,128)(2,1)} %bitcast.43, bf16[512,4,2,128]{3,2,1,0:T(2,128)(2,1)} %reshape.60), kind=kOutput, calls=%fused_computation.37 | convolution fusion | flops 1635780096 | bytes 3424256 | tf_op jit(solution)/shard_map/while/body/eval_jaxpr/sub | solution.py:78
  80.4 15.2 %fusion.10 = bf16[4,128,2,512]{3,1,2,0:T(8,128)(2,1)} fusion(bf16[1536,4,128,1]{0,2,3,1:T(8,128)(2,1)} %bitcast.44, f32[4,2,512]{2,1,0:T(2,128)S(1)} %fusion.30, f32[4,1536,512,2]{2,1,3,0:T(8,128)} %fusion.15, pred[512,1536]{0,1:T(8,128)(4,1)} %fusion.9), kind=kOutput, calls=%fused_computation.15 | convolution fusion | flops 1642599936 | bytes 28590080 | tf_op jit(solution)/shard_map/while/body/eval_jaxpr/kgql,lkd->qkgd/dot_general | solution.py:80
  95.6 2.3 %copy.18 = bf16[512,1024]{1,0:T(8,128)(2,1)} copy(bf16[512,1024]{0,1:T(8,128)(2,1)} %bitcast.45) | data formatting | bytes 2097152 | tf_op jit(solution)/shard_map/reshape | solution.py:84
  (3 shorter events, 0.0 us)
Async XLA Ops:
  0.0 3.1 %copy-start = (bf16[64,16,1344]{2,1,0:T(8,128)(2,1)S(1)}, bf16[64,16,1344]{2,1,0:T(8,128)(2,1)}, u32[]{:S(2)}) copy-start(bf16[64,16,1344]{2,1,0:T(8,128)(2,1)} %param.11) | copy-start | bytes 8257540
  23.8 12.9 %collective-permute-start = (bf16[512,512]{1,0:T(8,128)(2,1)}, bf16[512,512]{1,0:T(8,128)(2,1)}, u32[]{:S(2)}, u32[]{:S(2)}) collective-permute-start(bf16[512,512]{1,0:T(8,128)(2,1)} %fusion.11), channel_id=1, source_target_pairs={{0,4},{4,8},{8,12},{12,16},{16,20},{20,24},{24,28},{28,32},{32,36}... | collective-permute-start | bytes 1572872 | tf_op jit(solution)/shard_map/ppermute | solution.py:16
  27.0 15.4 %collective-permute-start.2 = (bf16[512,512]{0,1:T(8,128)(2,1)S(1)}, bf16[512,512]{0,1:T(8,128)(2,1)}, u32[]{:S(2)}, u32[]{:S(2)}) collective-permute-start(bf16[512,512]{0,1:T(8,128)(2,1)S(1)} %copy.12), channel_id=1, source_target_pairs={{0,4},{4,8},{8,12},{12,16},{16,20},{20,24},{24,28},{28,32},{32,36}... | collective-permute-start | bytes 1572872 | tf_op jit(solution)/shard_map/ppermute | solution.py:16
  36.7 12.9 %collective-permute-start.1 = (bf16[512,512]{1,0:T(8,128)(2,1)}, bf16[512,512]{1,0:T(8,128)(2,1)}, u32[]{:S(2)}, u32[]{:S(2)}) collective-permute-start(bf16[512,512]{1,0:T(8,128)(2,1)} %collective-permute-done), channel_id=1, source_target_pairs={{0,4},{4,8},{8,12},{12,16},{16,20},{20,24},{24,28},{28,32},{32,36}... | collective-permute-start | bytes 1572872 | tf_op jit(solution)/shard_map/ppermute | solution.py:16
  42.3 12.9 %collective-permute-start.3 = (bf16[512,512]{0,1:T(8,128)(2,1)}, bf16[512,512]{0,1:T(8,128)(2,1)}, u32[]{:S(2)}, u32[]{:S(2)}) collective-permute-start(bf16[512,512]{0,1:T(8,128)(2,1)} %collective-permute-done.2), channel_id=1, source_target_pairs={{0,4},{4,8},{8,12},{12,16},{16,20},{20,24},{24,28},{28,32},{32,36}... | collective-permute-start | bytes 1572872 | tf_op jit(solution)/shard_map/ppermute | solution.py:16
  54.9 2.8 %copy-start.2 = (bf16[512,4,2,128]{3,2,1,0:T(2,128)(2,1)S(1)}, bf16[512,4,2,128]{3,2,1,0:T(2,128)(2,1)}, u32[]{:S(2)}) copy-start(bf16[512,4,2,128]{3,2,1,0:T(2,128)(2,1)} %reshape.60) | copy-start | bytes 3145732
  56.6 1.1 %copy-start.1 = (bf16[1536,512]{0,1:T(8,128)(2,1)}, bf16[1536,512]{0,1:T(8,128)(2,1)S(1)}, u32[]{:S(2)}) copy-start(bf16[1536,512]{0,1:T(8,128)(2,1)S(1)} %pad_maximum_fusion.1) | copy-start | bytes 4718596
where the time goes:
time: 98.3 us; the launch traced here: 97.9 us
  matrix products  41.7 us (42%)
  blocking collectives  16.9 us (17%)
  local copies, waits for them, and re-layouts  11.3 us (11%)
  waiting for transfers between devices  10.7 us (11%)
  starting transfers between devices  9.66 us (10%)
  other arithmetic  5.86 us (6%)
  between operations  1.78 us (2%)
    psum x1, blocking collectives, on_device(): lax.psum(partial_value.reshape(tok, ADAPTER_RANK).astype(jnp.bfloat16), '...  16.9 us
    dot_general x1, matrix products, one_block(): jnp.einsum('kgql,lkd->qkgd', weights, vrows, preferred_element_type=jnp.f...  15.2 us
    dot_general x1, matrix products, one_block(): jnp.einsum('qkgd,lkd->kgql', qrows, krows, preferred_element_type=jnp.flo...  11.8 us
    sub x1, matrix products, one_block(): expo = jnp.exp(scores - top)  10.9 us
    ppermute x4, waiting for transfers between devices, shifted(): lax.ppermute(value, axis, [(source, source + steps) for source in range(l...  10.7 us
    ppermute x4, starting transfers between devices, shifted(): lax.ppermute(value, axis, [(source, source + steps) for source in range(l...  9.66 us
    reshape x1, local copies, waits for them, and re-layouts, one_block(): vrows = vals_all.reshape(span, kv_local, HEAD_WIDTH)  2.64 us
    concatenate x1, other arithmetic, on_device(): vals_all = jnp.concatenate(rim_vals + [value_full], axis=0)  2.61 us
  transfers between devices with their start and end apart: 4, of which 4 were waited for; matrix products, arithmetic and copies ran while one was open for 11% of the time, Pallas kernels for 0%

commit v1 on v0

--- a/solution.py
+++ b/solution.py
@@ -37,7 +37,9 @@
         selected_down,
         preferred_element_type=jnp.float32,
     )
-    rank_activation = lax.psum(partial_value.reshape(tok, ADAPTER_RANK).astype(jnp.bfloat16), "tp")
+    own = partial_value.reshape(tok, ADAPTER_RANK).astype(jnp.bfloat16)
+    parts = lax.all_gather(own, "tp", axis=0, tiled=False)
+    rank_activation = parts.sum(axis=0)
     hops = WINDOW // tok
     selected_up = adapter_up_maps[segment_adapter_ids]
     value_update = jnp.einsum(

time: 98.3 us -> 93.8 us (0.954)
  blocking collectives: 16.9 us -> 12.2 us
    psum x1 -> x0, blocking collectives: 16.9 us -> none  [on_device(): lax.psum(partial_value.reshape(tok, ADAPTER_RANK).astype(jnp.bfloat16), '...]
    all_gather x0 -> x1, blocking collectives: none -> 12.2 us  [on_device(): parts = lax.all_gather(own, 'tp', axis=0, tiled=False)]
  transfers between devices with their start and end apart: 4 -> 4, of which waited for: 4 -> 4; matrix products, arithmetic and copies ran while one was open for 11% -> 12% of each run, Pallas kernels for 0% -> 0%
where the time goes in v1:
time: 93.8 us; the launch traced here: 93.3 us
  matrix products  41.7 us (44%)
  blocking collectives  12.2 us (13%)
  local copies, waits for them, and re-layouts  11.3 us (12%)
  waiting for transfers between devices  10.7 us (11%)
  starting transfers between devices  9.65 us (10%)
  other arithmetic  5.95 us (6%)
  between operations  1.79 us (2%)
    dot_general x1, matrix products, one_block(): jnp.einsum('kgql,lkd->qkgd', weights, vrows, preferred_element_type=jnp.f...  15.2 us
    all_gather x1, blocking collectives, on_device(): parts = lax.all_gather(own, 'tp', axis=0, tiled=False)  12.2 us
    dot_general x1, matrix products, one_block(): jnp.einsum('qkgd,lkd->kgql', qrows, krows, preferred_element_type=jnp.flo...  11.8 us
    sub x1, matrix products, one_block(): expo = jnp.exp(scores - top)  10.9 us
    ppermute x4, waiting for transfers between devices, shifted(): lax.ppermute(value, axis, [(source, source + steps) for source in range(l...  10.7 us
    ppermute x4, starting transfers between devices, shifted(): lax.ppermute(value, axis, [(source, source + steps) for source in range(l...  9.65 us
    reshape x1, local copies, waits for them, and re-layouts, one_block(): vrows = vals_all.reshape(span, kv_local, HEAD_WIDTH)  2.64 us
    concatenate x1, other arithmetic, on_device(): vals_all = jnp.concatenate(rim_vals + [value_full], axis=0)  2.61 us
  transfers between devices with their start and end apart: 4, of which 4 were waited for; matrix products, arithmetic and copies ran while one was open for 12% of the time, Pallas kernels for 0%

profile of v1, /device:TPU:16, one launch (start us, length us, event | category | flops | bytes accessed | tf_op | source)
XLA Modules:
  0.0 93.3 jit_solution(9298967693171076130)
XLA Ops:
  0.0 0.0 copy-start
  0.0 1.4 %dynamic-slice.8 = s32[1]{0:T(128)} dynamic-slice(s32[16]{0:T(128)} %param.13, s32[]{:T(128)} %bitcast.1), dynamic_slice_sizes={1} | dynamic-slice | bytes 12 | tf_op jit(solution)/shard_map/gather | solution.py:32
  3.1 0.0 copy-done
  3.1 1.6 %fusion.12 = bf16[512,16]{0,1:T(8,128)(2,1)S(1)} fusion(bf16[512,1344]{0,1:T(8,128)(2,1)} %param.7, bf16[64,16,1344]{2,1,0:T(8,128)(2,1)S(1)} %copy-done, s32[]{:T(128)} %bitcast.2), kind=kOutput, calls=%fused_computation.19 | convolution fusion | flops 22028288 | bytes 1437700 | tf_op jit(solution)/shard_map/bsd,brd->bsr/dot_general | solution.py:34
  4.7 12.2 %all-gather = bf16[2048,16]{0,1:T(8,128)(2,1)S(1)} all-gather(bf16[512,16]{0,1:T(8,128)(2,1)S(1)} %fusion.12), channel_id=2, replica_groups=mesh['seq'=64,'tp'=4] {'tp'}, dimensions={0}, use_global_device_ids=true | all-gather | bytes 81920 | tf_op jit(solution)/shard_map/all_gather | solution.py:41
  17.0 0.1 reduce_sum.22
  17.0 2.2 %fusion.11 = bf16[512,512]{1,0:T(8,128)(2,1)} fusion(bf16[512,16]{0,1:T(8,128)(2,1)S(1)} %reduce_sum.22, bf16[512,512]{1,0:T(8,128)(2,1)} %param.10, bf16[64,16,512]{2,1,0:T(8,128)(2,1)} %param.12, s32[]{:T(128)} %bitcast.2), kind=kOutput, calls=%fused_computation.17 | convolution fusion | flops 9175040 | bytes 1081856 | tf_op jit(solution)/shard_map/bsr,brc->bsc/dot_general | solution.py:45
  19.2 1.9 %collective-permute-start = (bf16[512,512]{1,0:T(8,128)(2,1)}, bf16[512,512]{1,0:T(8,128)(2,1)}, u32[]{:S(2)}, u32[]{:S(2)}) collective-permute-start(bf16[512,512]{1,0:T(8,128)(2,1)} %fusion.11), channel_id=1, source_target_pairs={{0,4},{4,8},{8,12},{12,16},{16,20},{20,24},{24,28},{28,32},{32,36}... | collective-permute-start | bytes 1572872 | tf_op jit(solution)/shard_map/ppermute | solution.py:16
  21.2 1.3 %copy.19 = bf16[512,512]{0,1:T(8,128)(2,1)S(1)} copy(bf16[512,512]{1,0:T(8,128)(2,1)} %param.9) | data formatting | bytes 1048576 | tf_op args[2]
  22.4 3.9 %collective-permute-start.2 = (bf16[512,512]{0,1:T(8,128)(2,1)S(1)}, bf16[512,512]{0,1:T(8,128)(2,1)}, u32[]{:S(2)}, u32[]{:S(2)}) collective-permute-start(bf16[512,512]{0,1:T(8,128)(2,1)S(1)} %copy.19), channel_id=1, source_target_pairs={{0,4},{4,8},{8,12},{12,16},{16,20},{20,24},{24,28},{28,32},{32,36}... | collective-permute-start | bytes 1572872 | tf_op jit(solution)/shard_map/ppermute | solution.py:16
  26.4 5.8 %collective-permute-done = bf16[512,512]{1,0:T(8,128)(2,1)} collective-permute-done((bf16[512,512]{1,0:T(8,128)(2,1)}, bf16[512,512]{1,0:T(8,128)(2,1)}, u32[]{:S(2)}, u32[]{:S(2)}) %collective-permute-start) | collective-permute-done | bytes 524320 | tf_op jit(solution)/shard_map/ppermute | solution.py:16
  32.2 1.9 %collective-permute-start.1 = (bf16[512,512]{1,0:T(8,128)(2,1)}, bf16[512,512]{1,0:T(8,128)(2,1)}, u32[]{:S(2)}, u32[]{:S(2)}) collective-permute-start(bf16[512,512]{1,0:T(8,128)(2,1)} %collective-permute-done), channel_id=1, source_target_pairs={{0,4},{4,8},{8,12},{12,16},{16,20},{20,24},{24,28},{28,32},{32,36}... | collective-permute-start | bytes 1572872 | tf_op jit(solution)/shard_map/ppermute | solution.py:16
  34.1 2.6 %reshape.62 = bf16[512,4,2,128]{3,2,1,0:T(2,128)(2,1)} reshape(bf16[512,1024]{1,0:T(8,128)(2,1)} %param.8) | data formatting | bytes 2097152 | tf_op jit(solution)/shard_map/while/body/eval_jaxpr/reshape | solution.py:68
  36.7 1.1 %collective-permute-done.2 = bf16[512,512]{0,1:T(8,128)(2,1)} collective-permute-done((bf16[512,512]{0,1:T(8,128)(2,1)S(1)}, bf16[512,512]{0,1:T(8,128)(2,1)}, u32[]{:S(2)}, u32[]{:S(2)}) %collective-permute-start.2) | collective-permute-done | bytes 524320 | tf_op jit(solution)/shard_map/ppermute | solution.py:16
  37.8 1.9 %collective-permute-start.3 = (bf16[512,512]{0,1:T(8,128)(2,1)}, bf16[512,512]{0,1:T(8,128)(2,1)}, u32[]{:S(2)}, u32[]{:S(2)}) collective-permute-start(bf16[512,512]{0,1:T(8,128)(2,1)} %collective-permute-done.2), channel_id=1, source_target_pairs={{0,4},{4,8},{8,12},{12,16},{16,20},{20,24},{24,28},{28,32},{32,36}... | collective-permute-start | bytes 1572872 | tf_op jit(solution)/shard_map/ppermute | solution.py:16
  39.7 1.9 %fusion.9 = pred[512,1536]{0,1:T(8,128)(4,1)} fusion(s32[512]{0:T(512)S(1)} %iota_add_fusion.1, s32[1536]{0:T(1024)S(1)} %iota_add_fusion, pred[1536]{0:T(1024)(128)(4,1)S(1)} %broadcast_compare_fusion), kind=kLoop, calls=%fused_computation.12 | loop fusion | flops 3932160 | bytes 796160 | tf_op jit(solution)/shard_map/while/body/eval_jaxpr/and | solution.py:77
  41.6 3.5 %collective-permute-done.1 = bf16[512,512]{1,0:T(8,128)(2,1)} collective-permute-done((bf16[512,512]{1,0:T(8,128)(2,1)}, bf16[512,512]{1,0:T(8,128)(2,1)}, u32[]{:S(2)}, u32[]{:S(2)}) %collective-permute-start.1) | collective-permute-done | bytes 524320 | tf_op jit(solution)/shard_map/ppermute | solution.py:16
  45.1 2.6 %pad_maximum_fusion = bf16[1536,512]{1,0:T(8,128)(2,1)} fusion(bf16[512,512]{1,0:T(8,128)(2,1)} %fusion.11, bf16[512,512]{1,0:T(8,128)(2,1)} %collective-permute-done, bf16[512,512]{1,0:T(8,128)(2,1)} %collective-permute-done.1), kind=kLoop, calls=%fused_computation.13 | loop fusion | flops 4718592 | bytes 3145728 | tf_op jit(solution)/shard_map/concatenate | solution.py:61
  47.7 2.6 %copy.29 = bf16[1536,512]{0,1:T(8,128)(2,1)} copy(bf16[1536,512]{1,0:T(8,128)(2,1)} %pad_maximum_fusion) | data formatting | bytes 3145728 | tf_op jit(solution)/shard_map/while/body/eval_jaxpr/reshape | solution.py:70
  50.3 0.0 copy-start.2
  50.3 0.4 collective-permute-done.3
  50.7 1.3 %pad_maximum_fusion.1 = bf16[1536,512]{0,1:T(8,128)(2,1)S(1)} fusion(bf16[512,512]{0,1:T(8,128)(2,1)S(1)} %copy.19, bf16[512,512]{0,1:T(8,128)(2,1)} %collective-permute-done.2, bf16[512,512]{0,1:T(8,128)(2,1)} %collective-permute-done.3), kind=kLoop, calls=%fused_computation.14 | loop fusion | flops 4718592 | bytes 3145728 | tf_op jit(solution)/shard_map/concatenate | solution.py:60
  52.0 0.0 copy-start.1
  52.0 1.1 %copy-done.1 = bf16[1536,512]{0,1:T(8,128)(2,1)} copy-done((bf16[1536,512]{0,1:T(8,128)(2,1)}, bf16[1536,512]{0,1:T(8,128)(2,1)S(1)}, u32[]{:S(2)}) %copy-start.1) | copy-done | bytes 1572888
  53.2 0.0 copy-done.2
  53.2 11.8 %fusion.15 = f32[4,1536,512,2]{2,1,3,0:T(8,128)} fusion(bf16[1536,4,128,1]{0,2,3,1:T(8,128)(2,1)S(1)} %bitcast.44, bf16[512,4,2,128]{3,2,1,0:T(2,128)(2,1)S(1)} %copy-done.2), kind=kOutput, calls=%fused_computation.21 | convolution fusion | flops 1610612736 | bytes 27787264 | tf_op jit(solution)/shard_map/while/body/eval_jaxpr/qkgd,lkd->kgql/dot_general | solution.py:72
  64.9 10.9 %fusion.30 = f32[4,2,512]{2,1,0:T(2,128)S(1)} fusion(pred[512,1536]{0,1:T(8,128)(4,1)} %fusion.9, bf16[1536,4,128,1]{0,2,3,1:T(8,128)(2,1)} %bitcast.45, bf16[512,4,2,128]{3,2,1,0:T(2,128)(2,1)} %reshape.62), kind=kOutput, calls=%fused_computation.37 | convolution fusion | flops 1635780096 | bytes 3424256 | tf_op jit(solution)/shard_map/while/body/eval_jaxpr/sub | solution.py:80
  75.8 15.2 %fusion.10 = bf16[4,128,2,512]{3,1,2,0:T(8,128)(2,1)} fusion(bf16[1536,4,128,1]{0,2,3,1:T(8,128)(2,1)} %bitcast.46, f32[4,2,512]{2,1,0:T(2,128)S(1)} %fusion.30, f32[4,1536,512,2]{2,1,3,0:T(8,128)} %fusion.15, pred[512,1536]{0,1:T(8,128)(4,1)} %fusion.9), kind=kOutput, calls=%fused_computation.15 | convolution fusion | flops 1642599936 | bytes 28590080 | tf_op jit(solution)/shard_map/while/body/eval_jaxpr/kgql,lkd->qkgd/dot_general | solution.py:82
  91.0 2.3 %copy.25 = bf16[512,1024]{1,0:T(8,128)(2,1)} copy(bf16[512,1024]{0,1:T(8,128)(2,1)} %bitcast.47) | data formatting | bytes 2097152 | tf_op jit(solution)/shard_map/reshape | solution.py:86
  (4 shorter events, 0.1 us)
Async XLA Ops:
  0.0 3.1 %copy-start = (bf16[64,16,1344]{2,1,0:T(8,128)(2,1)S(1)}, bf16[64,16,1344]{2,1,0:T(8,128)(2,1)}, u32[]{:S(2)}) copy-start(bf16[64,16,1344]{2,1,0:T(8,128)(2,1)} %param.11) | copy-start | bytes 8257540
  19.2 12.9 %collective-permute-start = (bf16[512,512]{1,0:T(8,128)(2,1)}, bf16[512,512]{1,0:T(8,128)(2,1)}, u32[]{:S(2)}, u32[]{:S(2)}) collective-permute-start(bf16[512,512]{1,0:T(8,128)(2,1)} %fusion.11), channel_id=1, source_target_pairs={{0,4},{4,8},{8,12},{12,16},{16,20},{20,24},{24,28},{28,32},{32,36}... | collective-permute-start | bytes 1572872 | tf_op jit(solution)/shard_map/ppermute | solution.py:16
  22.4 15.4 %collective-permute-start.2 = (bf16[512,512]{0,1:T(8,128)(2,1)S(1)}, bf16[512,512]{0,1:T(8,128)(2,1)}, u32[]{:S(2)}, u32[]{:S(2)}) collective-permute-start(bf16[512,512]{0,1:T(8,128)(2,1)S(1)} %copy.19), channel_id=1, source_target_pairs={{0,4},{4,8},{8,12},{12,16},{16,20},{20,24},{24,28},{28,32},{32,36}... | collective-permute-start | bytes 1572872 | tf_op jit(solution)/shard_map/ppermute | solution.py:16
  32.2 12.9 %collective-permute-start.1 = (bf16[512,512]{1,0:T(8,128)(2,1)}, bf16[512,512]{1,0:T(8,128)(2,1)}, u32[]{:S(2)}, u32[]{:S(2)}) collective-permute-start(bf16[512,512]{1,0:T(8,128)(2,1)} %collective-permute-done), channel_id=1, source_target_pairs={{0,4},{4,8},{8,12},{12,16},{16,20},{20,24},{24,28},{28,32},{32,36}... | collective-permute-start | bytes 1572872 | tf_op jit(solution)/shard_map/ppermute | solution.py:16
  37.8 12.9 %collective-permute-start.3 = (bf16[512,512]{0,1:T(8,128)(2,1)}, bf16[512,512]{0,1:T(8,128)(2,1)}, u32[]{:S(2)}, u32[]{:S(2)}) collective-permute-start(bf16[512,512]{0,1:T(8,128)(2,1)} %collective-permute-done.2), channel_id=1, source_target_pairs={{0,4},{4,8},{8,12},{12,16},{16,20},{20,24},{24,28},{28,32},{32,36}... | collective-permute-start | bytes 1572872 | tf_op jit(solution)/shard_map/ppermute | solution.py:16
  50.3 2.8 %copy-start.2 = (bf16[512,4,2,128]{3,2,1,0:T(2,128)(2,1)S(1)}, bf16[512,4,2,128]{3,2,1,0:T(2,128)(2,1)}, u32[]{:S(2)}) copy-start(bf16[512,4,2,128]{3,2,1,0:T(2,128)(2,1)} %reshape.62) | copy-start | bytes 3145732
  52.0 1.1 %copy-start.1 = (bf16[1536,512]{0,1:T(8,128)(2,1)}, bf16[1536,512]{0,1:T(8,128)(2,1)S(1)}, u32[]{:S(2)}) copy-start(bf16[1536,512]{0,1:T(8,128)(2,1)S(1)} %pad_maximum_fusion.1) | copy-start | bytes 4718596
